TPU v7x, 32 devices: a whole 2x2x4 slice. The times are simulated.
32 devices in a mesh: seq: 8 (over y, x, core), batch: 4 (over z).
Axes of the slice: x: 2, y: 2, z: 4, core: 2. Of those that a mesh axis runs over, the one named last changes fastest.
Arguments:
- stream_in: bfloat16 [16, 2048, 768], P('batch', 'seq'), may hold values from -6 to 6
- lengths: int32 [16], P('batch'), may hold values from 64 to 2048, as said below
- token_mask: int32 [16, 2048], P('batch', 'seq'), may hold values from 0 to 1, as said below
- norm1_gain: bfloat16 [768], replicated, may hold values from 0.5 to 1.5
- w_qkv: bfloat16 [768, 2304], replicated, may hold values from -0.21875 to 0.21875
- conv_taps: bfloat16 [3, 2304], replicated, may hold values from -3 to 3
- w_out: bfloat16 [768, 768], replicated, may hold values from -1.75 to 1.75
- norm2_gain: bfloat16 [768], replicated, may hold values from 0.5 to 1.5
- w_up: bfloat16 [768, 3072], replicated, may hold values from -0.21875 to 0.21875
- w_down: bfloat16 [3072, 768], replicated, may hold values from -0.109375 to 0.109375
- grad_output: bfloat16 [16, 2048, 768], P('batch', 'seq'), may hold values from -6 to 6
Outputs:
- stream_out: bfloat16 [16, 2048, 768], P('batch', 'seq')
- grad_input: float32 [16, 2048, 768], P('batch', 'seq')
- grad_norm1: float32 [768], P('batch')
- grad_qkv: float32 [768, 2304], P('batch')
- grad_taps: float32 [3, 2304], replicated
- grad_wout: float32 [768, 768], P('batch')
- grad_norm2: float32 [768], P('batch')
- grad_up: float32 [768, 3072], P('batch')
- grad_down: float32 [3072, 768], P('batch')
- block_rms: float32 [3], replicated
Inputs may be any that keep to these rules, and one draw needn't show every extreme that they name: `lengths`: lengths are heavy tailed over 64 to 2048; some sequence has exactly 2048. `token_mask`: 0 or 1; the first position of every sequence is 1.
All inputs are finite; a program needn't handle non-finite values.
Results may differ from a plain program's by a relative error of at most 0.02.
Values may be sent and summed in bfloat16 or wider, within the bound.
A program may use at most 384 MiB of HBM per device.

v0:
```python
import functools
import math

import jax
import jax.numpy as jnp
from jax import lax
from jax.experimental import pallas as pl
from jax.experimental.pallas import tpu as pltpu
from jax.sharding import PartitionSpec as P

HEADS = 12
HEAD = 64
PAIRS = HEADS // 2
WIDE = 2 * HEAD
TILE = 256
ROWS = 512
BACK = 256
STRIP = 32
LIMIT = 62 << 20
NEG = -1e30
F32 = jnp.float32
BF16 = jnp.bfloat16


def mm(left_op, right_op):
    return jnp.dot(left_op, right_op, preferred_element_type=F32)


def mm_nt(left_op, right_op):
    return lax.dot_general(
        left_op, right_op, (((1,), (1,)), ((), ())), preferred_element_type=F32
    )


def mm_tn(left_op, right_op):
    return lax.dot_general(
        left_op, right_op, (((0,), (0,)), ((), ())), preferred_element_type=F32
    )


def params():
    return pltpu.CompilerParams(vmem_limit_bytes=LIMIT)


MESH = pl.DeviceIdType.MESH
GROUP = 8
DMA = pltpu.SemaphoreType.DMA


def remote(source, target, sems, axis, peer):
    return pltpu.make_async_remote_copy(
        src_ref=source,
        dst_ref=target,
        send_sem=sems[0],
        recv_sem=sems[1],
        device_id={axis: peer},
        device_id_type=MESH,
    )


def meet_group():
    me = lax.axis_index("seq")
    barrier = pltpu.get_barrier_semaphore()
    for bit in range(1, GROUP):
        pl.semaphore_signal(barrier, inc=1, device_id={"seq": me ^ bit}, device_id_type=MESH)
    pl.semaphore_wait(barrier, GROUP - 1)


def unit_copy(blocks, inbox, sems, unit):
    me = lax.axis_index("seq")
    owner, slot = lax.rem(unit, GROUP), unit // GROUP
    return owner, remote(
        blocks.at[unit],
        inbox.at[slot, me],
        (sems[0].at[unit], sems[1].at[slot, me ^ owner]),
        "seq",
        owner,
    )


def send_unit(blocks, inbox, sems, unit):
    me = lax.axis_index("seq")
    owner, copy = unit_copy(blocks, inbox, sems, unit)

    @pl.when(owner != me)
    def _():
        copy.start()

    @pl.when(owner == me)
    def _():
        slot = unit // GROUP
        pltpu.make_async_copy(blocks.at[unit], inbox.at[slot, me], sems[1].at[slot, 0]).start()


def wait_unit(blocks, inbox, sems, slot):
    me = lax.axis_index("seq")
    unit = slot * GROUP + me
    pltpu.make_async_copy(blocks.at[unit], inbox.at[slot, me], sems[1].at[slot, 0]).wait()
    for bit in range(1, GROUP):
        remote(
            blocks.at[unit],
            inbox.at[slot, me ^ bit],
            (sems[0].at[unit], sems[1].at[slot, bit]),
            "seq",
            me ^ bit,
        ).wait_recv()


def wait_sent(blocks, inbox, sems):
    me = lax.axis_index("seq")

    def one(unit, carry):
        owner, copy = unit_copy(blocks, inbox, sems, unit)
        pl.when(owner != me)(copy.wait_send)
        return carry

    lax.fori_loop(0, blocks.shape[0], one, 0)


def wait_units(blocks, inbox, sems):
    for slot in range(blocks.shape[0] // GROUP):
        wait_unit(blocks, inbox, sems, slot)
    wait_sent(blocks, inbox, sems)


def block_copies(units, inbox, sems, slot):
    me = lax.axis_index("seq")
    return [
        remote(
            units.at[slot, me ^ bit],
            inbox.at[slot * GROUP + me],
            (sems[0].at[slot, bit], sems[1].at[slot, bit]),
            "seq",
            me ^ bit,
        )
        for bit in range(1, GROUP)
    ]


def own_block(units, inbox, sems, slot):
    me = lax.axis_index("seq")
    return pltpu.make_async_copy(
        units.at[slot, me], inbox.at[slot * GROUP + me], sems[1].at[slot, 0]
    )


def send_blocks(units, inbox, sems, slot):
    own_block(units, inbox, sems, slot).start()
    for copy in block_copies(units, inbox, sems, slot):
        copy.start()


def wait_blocks(units, inbox, sems, slot):
    own_block(units, inbox, sems, slot).wait()
    for copy in block_copies(units, inbox, sems, slot):
        copy.wait()


def group_params(number):
    return pltpu.CompilerParams(
        collective_id=number, has_side_effects=True, vmem_limit_bytes=LIMIT
    )


def gain_row(gain_ref):
    return gain_ref[...].astype(F32).reshape(1, gain_ref.shape[0])


def project_kernel(x_ref, gain_ref, w_ref, n_ref, p_ref):
    x = x_ref[0].astype(F32)
    factor = lax.rsqrt(jnp.mean(x * x, axis=-1, keepdims=True) + 1e-06)
    normed = (x * factor * gain_row(gain_ref)).astype(BF16)
    n_ref[0] = normed
    width = x.shape[1]
    for part in range(3):
        cols = mm(normed, w_ref[:, part * width : (part + 1) * width])
        for pair in range(PAIRS):
            p_ref[pair, :, part * WIDE : (part + 1) * WIDE] = cols[
                :, pair * WIDE : (pair + 1) * WIDE
            ].astype(BF16)


def project(x, gain, w_qkv):
    groups, rows, width = x.shape
    return pl.pallas_call(
        project_kernel,
        grid=(groups,),
        in_specs=[
            pl.BlockSpec((1, rows, width), lambda s: (s, 0, 0)),
            pl.BlockSpec((width,), lambda s: (0,)),
            pl.BlockSpec(w_qkv.shape, lambda s: (0, 0)),
        ],
        out_specs=[
            pl.BlockSpec((1, rows, width), lambda s: (s, 0, 0)),
            pl.BlockSpec((PAIRS, rows, 3 * WIDE), lambda s: (s, 0, 0)),
        ],
        out_shape=[
            jax.ShapeDtypeStruct(x.shape, BF16),
            jax.ShapeDtypeStruct((groups * PAIRS, rows, 3 * WIDE), BF16),
        ],
        compiler_params=params(),
        name="project",
    )(x, gain, w_qkv)


def stack_heads(rows):
    lane = lax.broadcasted_iota(jnp.int32, rows.shape, 1)
    zero = jnp.zeros_like(rows)
    first = jnp.where(lane < HEAD, rows, zero)
    second = jnp.where(lane < HEAD, zero, rows)
    return jnp.concatenate([first, second], axis=0)


def unstack_heads(rows):
    half = rows.shape[0] // 2
    lane = lax.broadcasted_iota(jnp.int32, (half, rows.shape[1]), 1)
    return jnp.where(lane < HEAD, rows[:half], rows[half:])


def step_rows(index, size):
    return pl.ds(pl.multiple_of(index * size, size), size)


def own_unit(lengths, groups, count, slot):
    unit = slot * count + lax.axis_index("seq")
    length = lengths[jnp.minimum(unit // PAIRS, groups - 1)]
    return jnp.where(unit < groups * PAIRS, length, 0), lax.rem(unit, PAIRS)


def pair_taps(taps_ref, taps_sc, pair):
    width = taps_ref.shape[1] // 3
    for part in range(3):
        cols = pl.ds(pl.multiple_of(part * width + pair * WIDE, WIDE), WIDE)
        taps_sc[0:3, part * WIDE : (part + 1) * WIDE] = taps_ref[:, cols].astype(F32)


def convolve(wide_ref, taps_ref, tile, cols):
    begin = 8 + tile * TILE
    total = taps_ref[0:1, cols] * wide_ref[begin : begin + TILE, cols]
    total += taps_ref[1:2, cols] * wide_ref[begin - 1 : begin - 1 + TILE, cols]
    total += taps_ref[2:3, cols] * wide_ref[begin - 2 : begin - 2 + TILE, cols]
    return total.astype(BF16)


Q_COLS, K_COLS, V_COLS = (slice(part * WIDE, (part + 1) * WIDE) for part in range(3))


def key_limits(index, length, size):
    lane = lax.broadcasted_iota(jnp.int32, (STRIP, 2 * size), 1)
    return jnp.minimum(index * size + (lane & (size - 1)) + 1, length)


def over_key_steps(index, length, size, visit, carry):
    full = jnp.minimum(index * size, length) // size
    last = (jnp.minimum((index + 1) * size, length) + size - 1) // size
    carry = lax.fori_loop(0, full, lambda step, c: visit(step, False, c), carry)
    return lax.fori_loop(full, last, lambda step, c: visit(step, True, c), carry)


def attend_kernel(
    groups, count, lengths, p_ref, taps_ref, o_ref, lse_ref, taps, wide, q_sc, k_sc, vt_sc, acc, s_sc, e_sc
):
    length, pair = own_unit(lengths, groups, count, pl.program_id(0))
    wide[0:8] = jnp.zeros((8, wide.shape[1]), F32)
    wide[8:] = p_ref[0].astype(F32)
    attend_unit(
        length, pair, False, taps_ref, o_ref.at[0], lse_ref.at[0], taps, wide, q_sc, k_sc, vt_sc, acc, s_sc, e_sc
    )


def attend_unit(
    length, pair, whole, taps_ref, o_ref, lse_ref, taps, wide, q_sc, k_sc, vt_sc, acc, s_sc, e_sc
):
    tiles = q_sc.shape[0] // TILE
    per_step = ROWS // TILE
    pair_taps(taps_ref, taps, pair)
    vt_sc[:, WIDE:] = jnp.ones((vt_sc.shape[0], vt_sc.shape[1] - WIDE, ROWS), BF16)
    for tile in range(tiles):
        rows = slice(tile * TILE, (tile + 1) * TILE)
        q_sc[rows] = convolve(wide, taps, tile, Q_COLS) * (1.0 / math.sqrt(HEAD))

        def keys_values():
            k_sc[rows] = convolve(wide, taps, tile, K_COLS)
            cols = slice(tile % per_step * TILE, (tile % per_step + 1) * TILE)
            values = convolve(wide, taps, tile, V_COLS)
            vt_sc[tile // per_step, :WIDE, cols] = values.astype(F32).T.astype(BF16)

        if whole:
            keys_values()
        else:
            pl.when(tile // per_step * ROWS < length)(keys_values)

    k_row = lax.broadcasted_iota(jnp.int32, (STRIP, 2 * ROWS), 0)

    def query_step(index, carry):
        q_stack = stack_heads(q_sc[step_rows(index, ROWS)])
        limit = key_limits(index, length, ROWS)
        acc[...] = jnp.zeros(acc.shape, F32)

        def visit(step, mask, old):
            s_sc[...] = mm_nt(k_sc[step_rows(step, ROWS)], q_stack)

            def strip_of(begin):
                scores = s_sc[begin : begin + STRIP]
                if mask == "none":
                    return scores
                if mask == "length":
                    keep = k_row[:, :WIDE] < length - (step * ROWS + begin)
                    keep = jnp.concatenate([keep] * (2 * ROWS // WIDE), axis=1)
                else:
                    keep = k_row < limit - (step * ROWS + begin)
                return jnp.where(keep, scores, NEG)

            top = jnp.full((8, 2 * ROWS), NEG, F32)
            for begin in range(0, ROWS, STRIP):
                scores = strip_of(begin)
                for low in range(0, STRIP, 8):
                    top = jnp.maximum(top, scores[low : low + 8])
            new = jnp.maximum(old, jnp.max(top, axis=0, keepdims=True))
            for begin in range(0, ROWS, STRIP):
                e_sc[begin : begin + STRIP] = jnp.exp(strip_of(begin) - new).astype(BF16)
            acc[...] = acc[...] * jnp.exp(old - new) + mm(vt_sc[step], e_sc[...])
            return new

        top = jnp.full((1, 2 * ROWS), NEG, F32)
        if whole:
            top = lax.fori_loop(0, index, lambda step, c: visit(step, "length", c), top)
            top = visit(index, "both", top)
        else:

            def either(step, masked, top):
                return visit(step, "both" if masked else "none", top)

            top = over_key_steps(index, length, ROWS, either, top)
        total = acc[WIDE : WIDE + 1]
        out = (acc[:WIDE] / total).T
        o_ref[step_rows(index, ROWS)] = unstack_heads(out).astype(BF16)
        lse_ref[pl.ds(index, 1)] = top + jnp.log(total)
        return carry

    lax.fori_loop(0, q_sc.shape[0] // ROWS, query_step, 0)


def attend(lengths, proj, taps, count):
    slots, rows = proj.shape[:2]
    steps = rows // ROWS
    own = lambda i, lengths: (i, 0, 0)
    return pl.pallas_call(
        functools.partial(attend_kernel, lengths.shape[0], count),
        grid_spec=pltpu.PrefetchScalarGridSpec(
            num_scalar_prefetch=1,
            grid=(slots,),
            in_specs=[
                pl.BlockSpec((1, rows, 3 * WIDE), own),
                pl.BlockSpec(taps.shape, lambda i, lengths: (0, 0)),
            ],
            out_specs=[
                pl.BlockSpec((1, rows, WIDE), own),
                pl.BlockSpec((1, steps, 2 * ROWS), own),
            ],
            scratch_shapes=[
                pltpu.VMEM((8, 3 * WIDE), F32),
                pltpu.VMEM((rows + 8, 3 * WIDE), F32),
                pltpu.VMEM((rows, WIDE), BF16),
                pltpu.VMEM((rows, WIDE), BF16),
                pltpu.VMEM((steps, WIDE + 16, ROWS), BF16),
                pltpu.VMEM((WIDE + 16, 2 * ROWS), F32),
                pltpu.VMEM((ROWS, 2 * ROWS), F32),
                pltpu.VMEM((ROWS, 2 * ROWS), BF16),
            ],
        ),
        out_shape=[
            jax.ShapeDtypeStruct((slots, rows, WIDE), BF16),
            jax.ShapeDtypeStruct((slots, steps, 2 * ROWS), F32),
        ],
        compiler_params=params(),
        name="attend",
    )(lengths, proj, taps)


def row_copies(units, inbox, sems, slot, block):
    me = lax.axis_index("seq")
    return [
        remote(
            units.at[slot, pl.ds(pl.multiple_of((me ^ bit) * block, block), block)],
            inbox.at[slot * GROUP + me],
            (sems[0].at[slot, bit], sems[1].at[slot, bit]),
            "seq",
            me ^ bit,
        )
        for bit in range(1, GROUP)
    ]


def own_rows(units, inbox, sems, slot, block):
    me = lax.axis_index("seq")
    return pltpu.make_async_copy(
        units.at[slot, pl.ds(pl.multiple_of(me * block, block), block)],
        inbox.at[slot * GROUP + me],
        sems[1].at[slot, 0],
    )


def send_rows(units, inbox, sems, slot, block):
    own_rows(units, inbox, sems, slot, block).start()
    for copy in row_copies(units, inbox, sems, slot, block):
        copy.start()


def wait_rows(units, inbox, sems, slot, block):
    own_rows(units, inbox, sems, slot, block).wait()
    for copy in row_copies(units, inbox, sems, slot, block):
        copy.wait()


def attend_back_kernel(
    groups, count, lengths, p_ref, taps_ref, o_ref, do_ref, lse_ref, dp_ref, gt_ref,
    taps, wide, q_sc, k_sc, v_sc, kt_sc, dm, dqt, s_sc, d_sc, e_sc, f_sc,
):
    p_ref, o_ref, do_ref, lse_ref = p_ref.at[0], o_ref.at[0], do_ref.at[0], lse_ref.at[0]
    dp_ref = dp_ref.at[0]
    length, pair = own_unit(lengths, groups, count, pl.program_id(0))
    tiles = p_ref.shape[0] // TILE
    per_step = BACK // TILE
    pair_taps(taps_ref, taps, pair)
    wide[0:8] = jnp.zeros((8, wide.shape[1]), F32)
    wide[8:] = p_ref[...].astype(F32)
    dm[...] = jnp.zeros(dm.shape, F32)
    for tile in range(tiles):
        rows = slice(tile * TILE, (tile + 1) * TILE)

        @pl.when(tile // per_step * BACK < length)
        def _():
            q_sc[rows] = convolve(wide, taps, tile, Q_COLS) * (1.0 / math.sqrt(HEAD))
            keys = convolve(wide, taps, tile, K_COLS)
            k_sc[rows] = keys
            v_sc[rows] = convolve(wide, taps, tile, V_COLS)
            cols = slice(tile % per_step * TILE, (tile % per_step + 1) * TILE)
            kt_sc[tile // per_step, :, cols] = keys.astype(F32).T.astype(BF16)

    lane = lax.broadcasted_iota(jnp.int32, (8, WIDE), 1)
    row = lax.broadcasted_iota(jnp.int32, (8, WIDE), 0)
    picks = jnp.where((lane < HEAD) == (row == 0), 1.0, 0.0).astype(BF16)
    k_row = lax.broadcasted_iota(jnp.int32, (STRIP, 2 * BACK), 0)

    def query_step(index, carry):
        here = step_rows(index, BACK)
        q_stack = stack_heads(q_sc[here])
        d_rows = do_ref[here]
        d_stack = stack_heads(d_rows)
        product = d_rows.astype(F32) * o_ref[here].astype(F32)
        upper = product.astype(BF16)
        lower = (product - upper.astype(F32)).astype(BF16)
        sums = mm_nt(picks, upper) + mm_nt(picks, lower)
        delta = jnp.concatenate([sums[0:1], sums[1:2]], axis=1)
        line, begin = pl.ds(index * BACK // ROWS, 1), lax.rem(index * BACK, ROWS)
        lse = jnp.concatenate(
            [
                lse_ref[line, pl.ds(pl.multiple_of(head * ROWS + begin, BACK), BACK)]
                for head in range(2)
            ],
            axis=1,
        )
        limit = key_limits(index, length, BACK)
        dqt[...] = jnp.zeros(dqt.shape, F32)

        def visit(step, masked, carry):
            there = step_rows(step, BACK)
            s_sc[...] = mm_nt(k_sc[there], q_stack)
            d_sc[...] = mm_nt(v_sc[there], d_stack)
            for begin in range(0, BACK, STRIP):
                strip = slice(begin, begin + STRIP)
                probs = jnp.exp(s_sc[strip] - lse)
                if masked:
                    probs = jnp.where(k_row < limit - (step * BACK + begin), probs, 0.0)
                e_sc[strip] = probs.astype(BF16)
                f_sc[strip] = (probs * (d_sc[strip] - delta)).astype(BF16)
            dm[there, V_COLS] += mm(e_sc[...], d_stack)
            dm[there, K_COLS] += mm(f_sc[...], q_stack)
            dqt[...] += mm(kt_sc[step], f_sc[...])
            return carry

        over_key_steps(index, length, BACK, visit, 0)
        dm[here, Q_COLS] = unstack_heads(dqt[...].T) * (1.0 / math.sqrt(HEAD))
        return carry

    lax.fori_loop(0, (length + BACK - 1) // BACK, query_step, 0)

    @pl.when(pl.program_id(0) == 0)
    def _():
        gt_ref[...] = jnp.zeros(gt_ref.shape, F32)

    sums = [jnp.zeros((1, 3 * WIDE), F32) for _ in range(3)]
    for tile in range(tiles):
        begin = tile * TILE
        total = taps[0:1] * dm[begin : begin + TILE]
        total += taps[1:2] * dm[begin + 1 : begin + 1 + TILE]
        total += taps[2:3] * dm[begin + 2 : begin + 2 + TILE]
        dp_ref[begin : begin + TILE] = total.astype(BF16)
        for tap in range(3):
            behind = wide[begin + 8 - tap : begin + 8 - tap + TILE]
            sums[tap] += jnp.sum(dm[begin : begin + TILE] * behind, axis=0, keepdims=True)
    width = gt_ref.shape[1] // 3
    for tap in range(3):
        for part in range(3):
            cols = pl.ds(pl.multiple_of(part * width + pair * WIDE, WIDE), WIDE)
            gt_ref[tap : tap + 1, cols] += sums[tap][:, part * WIDE : (part + 1) * WIDE]


def attend_back(lengths, proj, taps, attended, d_attended, lse, count):
    slots, rows = proj.shape[:2]
    steps = rows // BACK
    own = lambda i, lengths: (i, 0, 0)
    whole = lambda i, lengths: (0, 0)
    return pl.pallas_call(
        functools.partial(attend_back_kernel, lengths.shape[0], count),
        grid_spec=pltpu.PrefetchScalarGridSpec(
            num_scalar_prefetch=1,
            grid=(slots,),
            in_specs=[
                pl.BlockSpec((1, rows, 3 * WIDE), own),
                pl.BlockSpec(taps.shape, whole),
                pl.BlockSpec((1, rows, WIDE), own),
                pl.BlockSpec((1, rows, WIDE), own),
                pl.BlockSpec((1,) + lse.shape[1:], own),
            ],
            out_specs=[
                pl.BlockSpec((1, rows, 3 * WIDE), own),
                pl.BlockSpec((8, taps.shape[1]), whole),
            ],
            scratch_shapes=[
                pltpu.VMEM((8, 3 * WIDE), F32),
                pltpu.VMEM((rows + 8, 3 * WIDE), F32),
                pltpu.VMEM((rows, WIDE), BF16),
                pltpu.VMEM((rows, WIDE), BF16),
                pltpu.VMEM((rows, WIDE), BF16),
                pltpu.VMEM((steps, WIDE, BACK), BF16),
                pltpu.VMEM((rows + 8, 3 * WIDE), F32),
                pltpu.VMEM((WIDE, 2 * BACK), F32),
                pltpu.VMEM((BACK, 2 * BACK), F32),
                pltpu.VMEM((BACK, 2 * BACK), F32),
                pltpu.VMEM((BACK, 2 * BACK), BF16),
                pltpu.VMEM((BACK, 2 * BACK), BF16),
            ],
        ),
        out_shape=[
            jax.ShapeDtypeStruct((slots, rows, 3 * WIDE), BF16),
            jax.ShapeDtypeStruct((8, taps.shape[1]), F32),
        ],
        compiler_params=params(),
        name="attend_back",
    )(lengths, proj, taps, attended, d_attended, lse)


def dense_kernel(
    group, x_ref, att_ref, cot_ref, mask_ref, lengths, gain_ref, wo_ref, wu_ref, wd_ref,
    out_ref, dh_ref, datt_ref, n2_ref, sq_ref, du_ref, da_ref, cz_ref, gain_grad_ref, stats_ref,
    act_sc, att_sc,
):
    rows, width = x_ref.shape[1:]
    hidden_units = wu_ref.shape[1]
    step = width
    for pair in range(PAIRS):
        att_sc[:, pair * WIDE : (pair + 1) * WIDE] = att_ref[pair]
    spot = lax.axis_index("seq") * rows + lax.broadcasted_iota(jnp.int32, (1, rows), 1)
    counts = jnp.where(spot < lengths[group], mask_ref[pl.ds(group, 1)].astype(F32), 0.0)
    weight = jnp.broadcast_to(counts, (WIDE, rows)).T[:, :1]
    gain = gain_row(gain_ref)
    branch = mm(att_sc[...], wo_ref[...])
    hidden = x_ref[0].astype(F32) + branch
    factor = lax.rsqrt(jnp.mean(hidden * hidden, axis=-1, keepdims=True) + 1e-06)
    normed = (hidden * factor * gain).astype(BF16)
    n2_ref[0] = normed
    total = jnp.zeros((rows, width), F32)
    for begin in range(0, hidden_units, step):
        cols = slice(begin, begin + step)
        active = jnp.maximum(mm(normed, wu_ref[:, cols]), 0.0)
        act_sc[:, cols] = active
        squared = (active * active).astype(BF16)
        sq_ref[0, :, cols] = squared
        total += mm(squared, wd_ref[cols])
    full = hidden + total
    out_ref[0] = full.astype(BF16)

    def masked(values):
        per_row = jnp.sum(values * values, axis=-1, keepdims=True)
        return jnp.sum(weight * per_row, axis=0, keepdims=True)

    @pl.when(group == 0)
    def _():
        stats_ref[...] = jnp.zeros(stats_ref.shape, F32)
        gain_grad_ref[...] = jnp.zeros(gain_grad_ref.shape, F32)

    parts = [masked(full), masked(branch), masked(total), jnp.sum(weight, axis=0, keepdims=True)]
    for place, part in enumerate(parts):
        stats_ref[place : place + 1] += jnp.broadcast_to(part, (1, WIDE))
    cotangent = (cot_ref[0].astype(F32) * weight).astype(BF16)
    cz_ref[0] = cotangent
    d_normed = jnp.zeros((rows, width), F32)
    for begin in range(0, hidden_units, step):
        cols = slice(begin, begin + step)
        d_squared = mm_nt(cotangent, wd_ref[cols])
        d_up = (2.0 * act_sc[:, cols] * d_squared).astype(BF16)
        du_ref[0, :, cols] = d_up
        d_normed += mm_nt(d_up, wu_ref[:, cols])
    weighted = d_normed * gain
    inner = jnp.mean(weighted * hidden, axis=-1, keepdims=True)
    d_hidden = cotangent.astype(F32) + factor * weighted - hidden * (factor * factor * factor) * inner
    gain_grad_ref[...] += jnp.sum(d_normed * hidden * factor, axis=0, keepdims=True)
    dh_ref[0] = d_hidden
    d_attn = d_hidden.astype(BF16)
    da_ref[0] = d_attn
    d_att = mm_nt(d_attn, wo_ref[...]).astype(BF16)
    for pair in range(PAIRS):
        datt_ref[pair] = d_att[:, pair * WIDE : (pair + 1) * WIDE]


def dense(x, attended, grad_output, token_mask, lengths, gain, w_out, w_up, w_down):
    groups, rows, width = x.shape
    hidden_units = w_up.shape[1]
    per_group = lambda s: (s, 0, 0)
    fixed = lambda s: (0, 0)
    once = pl.Buffered(1)
    row_block = pl.BlockSpec((1, rows, width), per_group)
    wide_block = pl.BlockSpec((1, rows, hidden_units), per_group)
    unit_block = pl.BlockSpec((PAIRS, rows, WIDE), per_group)
    low = jax.ShapeDtypeStruct(x.shape, BF16)
    wide_low = jax.ShapeDtypeStruct((groups, rows, hidden_units), BF16)
    return pl.pallas_call(
        lambda *refs: dense_kernel(pl.program_id(0), *refs),
        grid=(groups,),
        in_specs=[
            row_block,
            unit_block,
            row_block,
            pl.BlockSpec(token_mask.shape, fixed),
            pl.BlockSpec(memory_space=pltpu.SMEM),
            pl.BlockSpec((width,), lambda s: (0,)),
            pl.BlockSpec(w_out.shape, fixed, pipeline_mode=once),
            pl.BlockSpec(w_up.shape, fixed, pipeline_mode=once),
            pl.BlockSpec(w_down.shape, fixed, pipeline_mode=once),
        ],
        out_specs=[
            row_block,
            row_block,
            unit_block,
            row_block,
            wide_block,
            wide_block,
            row_block,
            row_block,
            pl.BlockSpec((1, width), fixed),
            pl.BlockSpec((8, WIDE), fixed),
        ],
        out_shape=[
            low,
            jax.ShapeDtypeStruct(x.shape, F32),
            jax.ShapeDtypeStruct((groups * PAIRS, rows, WIDE), BF16),
            low,
            wide_low,
            wide_low,
            low,
            low,
            jax.ShapeDtypeStruct((1, width), F32),
            jax.ShapeDtypeStruct((8, WIDE), F32),
        ],
        scratch_shapes=[pltpu.VMEM((rows, hidden_units), F32), pltpu.VMEM((rows, width), BF16)],
        compiler_params=params(),
        name="dense",
    )(x, attended, grad_output, token_mask, lengths, gain, w_out, w_up, w_down)


def front_kernel(
    lengths, x_ref, gain_ref, w_ref, taps_ref, cot_ref, mask_ref, gain2_ref, wo_ref, wu_ref, wd_ref,
    n1_out, proj_out, units_out, att_out, lse_ref, inbox, gain_grad_ref, stats_ref,
    out_ref, dh_ref, n2_ref, sq_ref, du_ref, da_ref, cz_ref,
    x_v, w_v, n1_v, blocks, proj, units, att, taps, wide, q_sc, k_sc, vt_sc, acc, s_sc, e_sc,
    cot_v, wo_v, wu_v, wd_v, act_sc, att_sc, d_blocks,
    out_b, dh_b, n2_b, sq_b, du_b, da_b, cz_b,
    load_s, store_s, keep_s, send_s, send_r, att_s, att_r, back_s, back_r,
):
    groups, block = x_v.shape[:2]
    slots = proj.shape[0]
    sems, att_sems, back_sems = (send_s, send_r), (att_s, att_r), (back_s, back_r)
    loads = [
        pltpu.make_async_copy(source, target, load_s.at[place])
        for place, (source, target) in enumerate(
            [
                (w_ref, w_v),
                (x_ref, x_v),
                (wo_ref, wo_v),
                (wu_ref, wu_v),
                (wd_ref, wd_v),
                (cot_ref, cot_v),
            ]
        )
    ]
    keeps = [
        pltpu.make_async_copy(source, target, keep_s.at[place])
        for place, (source, target) in enumerate(
            [(n1_v, n1_out), (proj, proj_out), (units, units_out), (att, att_out)]
        )
    ]
    buffers = (out_b, dh_b, n2_b, sq_b, du_b, da_b, cz_b)
    targets = (out_ref, dh_ref, n2_ref, sq_ref, du_ref, da_ref, cz_ref)

    def stores(group):
        side = lax.rem(group, 2)
        return [
            pltpu.make_async_copy(buffer.at[side], target.at[group], store_s.at[place, side])
            for place, (buffer, target) in enumerate(zip(buffers, targets))
        ]

    for copy in loads:
        copy.start()
    meet_group()
    for copy in loads[:2]:
        copy.wait()

    def sequence(group, carry):
        here = pl.ds(group, 1)
        project_kernel(
            x_v.at[here], gain_ref, w_v, n1_v.at[here], blocks.at[pl.ds(group * PAIRS, PAIRS)]
        )
        for pair in range(PAIRS):
            send_unit(blocks, proj, sems, group * PAIRS + pair)
        return carry

    lax.fori_loop(0, groups, sequence, 0)
    keeps[0].start()

    def one_slot(slot, carry):
        wait_unit(blocks, proj, sems, slot)

        @pl.when(slot == slots - 1)
        def _():
            for done in range(slots - 1):
                send_rows(units, att, att_sems, done, block)

        length, pair = own_unit(lengths, groups, GROUP, slot)
        wide[0:8] = jnp.zeros((8, wide.shape[1]), F32)
        for place in range(GROUP):
            wide[8 + place * block : 8 + (place + 1) * block] = proj[slot, place].astype(F32)
        attend_unit(
            length, pair, True, taps_ref, units.at[slot], lse_ref.at[slot],
            taps, wide, q_sc, k_sc, vt_sc, acc, s_sc, e_sc,
        )
        return carry

    lax.fori_loop(0, slots, one_slot, 0)
    send_rows(units, att, att_sems, slots - 1, block)
    keeps[1].start()
    keeps[2].start()
    for copy in loads[2:]:
        copy.wait()

    def dense_group(group, carry):
        for slot in range(slots):

            @pl.when(group == slot * GROUP // PAIRS)
            def _():
                wait_rows(units, att, att_sems, slot, block)
                if slot == slots - 1:
                    keeps[3].start()

        @pl.when(group >= 2)
        def _():
            for copy in stores(group - 2):
                copy.wait()

        here, side = pl.ds(group, 1), pl.ds(lax.rem(group, 2), 1)
        unit = pl.ds(group * PAIRS, PAIRS)
        dense_kernel(
            group, x_v.at[here], att.at[unit], cot_v.at[here], mask_ref, lengths, gain2_ref,
            wo_v, wu_v, wd_v, out_b.at[side], dh_b.at[side], d_blocks.at[unit], n2_b.at[side],
            sq_b.at[side], du_b.at[side], da_b.at[side], cz_b.at[side], gain_grad_ref, stats_ref,
            act_sc, att_sc,
        )
        for pair in range(PAIRS):
            send_unit(d_blocks, inbox, back_sems, group * PAIRS + pair)
        for copy in stores(group):
            copy.start()
        return carry

    lax.fori_loop(0, groups, dense_group, 0)
    wait_sent(blocks, proj, sems)
    wait_units(d_blocks, inbox, back_sems)
    for group in (groups - 2, groups - 1):
        for copy in stores(group):
            copy.wait()
    for copy in keeps:
        copy.wait()


def front(x, gain, w_qkv, taps, lengths, grad_output, token_mask, gain2, w_out, w_up, w_down):
    groups, block, width = x.shape
    hidden_units = w_up.shape[1]
    units = groups * PAIRS
    slots = units // GROUP
    rows = GROUP * block
    steps = rows // ROWS
    anywhere = pl.BlockSpec(memory_space=pl.ANY)
    vmem = pl.BlockSpec(memory_space=pltpu.VMEM)
    low = lambda *shape: pltpu.VMEM(shape, BF16)
    low_out = lambda *shape: jax.ShapeDtypeStruct(shape, BF16)
    wide_out = (groups, block, hidden_units)
    return pl.pallas_call(
        front_kernel,
        in_specs=[pl.BlockSpec(memory_space=pltpu.SMEM), anywhere, vmem, anywhere, vmem]
        + [anywhere, vmem, vmem, anywhere, anywhere, anywhere],
        out_specs=[anywhere] * 4 + [vmem, anywhere, vmem, vmem] + [anywhere] * 7,
        out_shape=[
            low_out(*x.shape),
            low_out(slots, GROUP, block, 3 * WIDE),
            low_out(slots, rows, WIDE),
            low_out(units, block, WIDE),
            jax.ShapeDtypeStruct((slots, steps, 2 * ROWS), F32),
            low_out(slots, GROUP, block, WIDE),
            jax.ShapeDtypeStruct((1, width), F32),
            jax.ShapeDtypeStruct((8, WIDE), F32),
            low_out(*x.shape),
            jax.ShapeDtypeStruct(x.shape, F32),
            low_out(*x.shape),
            low_out(*wide_out),
            low_out(*wide_out),
            low_out(*x.shape),
            low_out(*x.shape),
        ],
        scratch_shapes=[
            low(*x.shape),
            low(*w_qkv.shape),
            low(*x.shape),
            low(units, block, 3 * WIDE),
            low(slots, GROUP, block, 3 * WIDE),
            low(slots, rows, WIDE),
            low(units, block, WIDE),
            pltpu.VMEM((8, 3 * WIDE), F32),
            pltpu.VMEM((rows + 8, 3 * WIDE), F32),
            low(rows, WIDE),
            low(rows, WIDE),
            low(steps, WIDE + 16, ROWS),
            pltpu.VMEM((WIDE + 16, 2 * ROWS), F32),
            pltpu.VMEM((ROWS, 2 * ROWS), F32),
            low(ROWS, 2 * ROWS),
            low(*x.shape),
            low(*w_out.shape),
            low(*w_up.shape),
            low(*w_down.shape),
            pltpu.VMEM((block, hidden_units), F32),
            low(block, width),
            low(units, block, WIDE),
            low(2, block, width),
            pltpu.VMEM((2, block, width), F32),
            low(2, block, width),
            low(2, block, hidden_units),
            low(2, block, hidden_units),
            low(2, block, width),
            low(2, block, width),
            DMA((6,)),
            DMA((7, 2)),
            DMA((4,)),
            DMA((units,)),
            DMA((slots, GROUP)),
            DMA((slots, GROUP)),
            DMA((slots, GROUP)),
            DMA((units,)),
            DMA((slots, GROUP)),
        ],
        compiler_params=group_params(1),
        name="front",
    )(lengths, x, gain, w_qkv, taps, grad_output, token_mask, gain2, w_out, w_up, w_down)


PART = 384
BY_CHIP = 288


def feed_grads_kernel(sq_ref, cz_ref, n2_ref, du_ref, att_ref, da_ref, out_ref, n2_t):
    half, sub = pl.program_id(0), pl.program_id(1)
    groups, rows, width = n2_ref.shape
    tokens = groups * rows

    @pl.when((half == 0) & (sub == 0))
    def _():
        for group in range(groups):
            n2_t[:, group * rows : (group + 1) * rows] = n2_ref[group].astype(F32).T.astype(BF16)

    down = mm_tn(sq_ref[...].reshape(tokens, PART), cz_ref[...].reshape(tokens, width))
    for place in range(4):
        for side in range(2):
            out_ref[place, pl.ds(sub, 1), side * 96 : side * 96 + 96] = down[
                place * 96 : (place + 1) * 96, side * PART : (side + 1) * PART
            ].astype(BF16)[None]
    up = mm(n2_t[...], du_ref[...].reshape(tokens, PART))
    out_ref[pl.ds(sub, 1), :, 192:384] = up.astype(BF16).reshape(1, 4, 192, PART)

    @pl.when(sub == 0)
    def _():
        att = jnp.concatenate(
            [att_ref[:, pair].reshape(tokens, WIDE) for pair in range(PAIRS)], axis=1
        )
        out = mm_tn(att, da_ref[...].reshape(tokens, PART)).astype(BF16)
        for batch in range(4):
            for q in range(4):
                begin = batch * 192 + q * 48
                out_ref[q, batch, 384:432] = out[begin : begin + 48]


def feed_grads(squared, cotangent, normed2, d_up, attended, d_attn):
    groups, rows, width = normed2.shape
    whole = lambda h, b: (0, 0, 0)
    return pl.pallas_call(
        feed_grads_kernel,
        grid=(2, 4),
        in_specs=[
            pl.BlockSpec((groups, rows, PART), lambda h, b: (0, 0, 2 * b + h)),
            pl.BlockSpec((groups, rows, width), whole, pipeline_mode=pl.Buffered(1)),
            pl.BlockSpec((groups, rows, width), whole, pipeline_mode=pl.Buffered(1)),
            pl.BlockSpec((groups, rows, PART), lambda h, b: (0, 0, 4 * h + b)),
            pl.BlockSpec(
                (groups, PAIRS, rows, WIDE), lambda h, b: (0, 0, 0, 0), pipeline_mode=pl.Buffered(1)
            ),
            pl.BlockSpec((groups, rows, PART), lambda h, b: (0, 0, h)),
        ],
        out_specs=pl.BlockSpec((4, 4, 432, PART), lambda h, b: (h, 0, 0, 0)),
        out_shape=jax.ShapeDtypeStruct((8, 4, 432, PART), BF16),
        scratch_shapes=[pltpu.VMEM((width, groups * rows), BF16)],
        compiler_params=params(),
        name="feed_grads",
    )(squared, cotangent, normed2, d_up, attended.reshape(groups, PAIRS, rows, WIDE), d_attn)


def feed_grads_send_kernel(
    sq_ref, cz_ref, n2_ref, du_ref, att_ref, da_ref, chip_ref, z_ref,
    n2_t, pieces, core_in, down_s, down_r, up_s, up_r, out_s, out_r,
):
    half, sub = pl.program_id(0), pl.program_id(1)
    me = lax.axis_index("seq")
    core = lax.rem(me, 2)
    other = 1 - core

    @pl.when((half == 0) & (sub == 0))
    def _():
        barrier = pltpu.get_barrier_semaphore()
        pl.semaphore_signal(barrier, inc=1, device_id={"seq": me ^ 1}, device_id_type=MESH)
        pl.semaphore_wait(barrier, 1)

    feed_grads_kernel(
        sq_ref, cz_ref, n2_ref, du_ref, att_ref, da_ref, pieces.at[pl.ds(half * 4, 4)], n2_t
    )

    def down(part, batch, side):
        chip = part * 2 + side
        return remote(
            pieces.at[chip * 2 + other, batch, 0:192],
            core_in.at[chip, batch, 0:192],
            (down_s.at[part, batch, side], down_r.at[part, batch, side]),
            "seq",
            me ^ 1,
        )

    def up(chip):
        return remote(
            pieces.at[chip * 2 + other, :, 192:384],
            core_in.at[chip, :, 192:384],
            (up_s.at[chip], up_r.at[chip]),
            "seq",
            me ^ 1,
        )

    def out(chip):
        return remote(
            pieces.at[chip * 2 + other, :, 384:432],
            core_in.at[chip, :, 384:432],
            (out_s.at[chip], out_r.at[chip]),
            "seq",
            me ^ 1,
        )

    for side in range(2):
        down(half, sub, side).start()

    @pl.when(sub == 0)
    def _():
        for side in range(2):
            out(half * 2 + side).start()

    @pl.when(lax.rem(sub, 2) == other)
    def _():
        up(half * 2 + sub // 2).start()

    @pl.when((half == 1) & (sub == 3))
    def _():
        for part in range(2):
            for side in range(2):
                chip = part * 2 + side
                for batch in range(4):
                    down(part, batch, side).wait()
                up(chip).wait()
                out(chip).wait()
                for batch in range(4):
                    both = pieces[chip * 2 + core, batch].astype(F32) + core_in[chip, batch].astype(F32)
                    chip_ref[chip, batch] = both[:BY_CHIP].astype(BF16)
                    z_ref[batch, chip] = both[BY_CHIP:].astype(BF16)


def feed_grads_send(squared, cotangent, normed2, d_up, attended, d_attn):
    groups, rows, width = normed2.shape
    whole = lambda h, b: (0, 0, 0)
    once = pl.Buffered(1)
    quarter = (4, 4, 432, PART)
    return pl.pallas_call(
        feed_grads_send_kernel,
        grid=(2, 4),
        in_specs=[
            pl.BlockSpec((groups, rows, PART), lambda h, b: (0, 0, 2 * b + h)),
            pl.BlockSpec((groups, rows, width), whole, pipeline_mode=once),
            pl.BlockSpec((groups, rows, width), whole, pipeline_mode=once),
            pl.BlockSpec((groups, rows, PART), lambda h, b: (0, 0, 4 * h + b)),
            pl.BlockSpec((groups, PAIRS, rows, WIDE), lambda h, b: (0, 0, 0, 0), pipeline_mode=once),
            pl.BlockSpec((groups, rows, PART), lambda h, b: (0, 0, h)),
        ],
        out_specs=[
            pl.BlockSpec((4, 4, BY_CHIP, PART), lambda h, b: (0, 0, 0, 0), pipeline_mode=once),
            pl.BlockSpec((4, 4, 432 - BY_CHIP, PART), lambda h, b: (0, 0, 0, 0), pipeline_mode=once),
        ],
        out_shape=[
            jax.ShapeDtypeStruct((4, 4, BY_CHIP, PART), BF16),
            jax.ShapeDtypeStruct((4, 4, 432 - BY_CHIP, PART), BF16),
        ],
        scratch_shapes=[
            pltpu.VMEM((width, groups * rows), BF16),
            pltpu.VMEM((8, 4, 432, PART), BF16),
            pltpu.VMEM(quarter, BF16),
            DMA((2, 4, 2)),
            DMA((2, 4, 2)),
            DMA((4,)),
            DMA((4,)),
            DMA((4,)),
            DMA((4,)),
        ],
        compiler_params=group_params(3),
        name="feed_grads_send",
    )(squared, cotangent, normed2, d_up, attended.reshape(groups, PAIRS, rows, WIDE), d_attn)


def input_grads_kernel(
    dp_ref, n1_ref, x_ref, dh_ref, w_ref, gain_ref, out_ref, gx_ref, gain_grad_ref, n1_t, total, w_sc
):
    pair = pl.program_id(0)
    groups, rows, width = n1_ref.shape
    tokens = groups * rows

    @pl.when(pair == 0)
    def _():
        for group in range(groups):
            n1_t[:, group * rows : (group + 1) * rows] = n1_ref[group].astype(F32).T.astype(BF16)
        total[...] = jnp.zeros(total.shape, F32)

    d_proj = dp_ref[...].reshape(tokens, 3 * WIDE)
    grad = mm(n1_t[...], d_proj).astype(BF16)
    for batch in range(4):
        for chip in range(4):
            begin = batch * 192 + chip * 48
            out_ref[0, 0, chip, batch] = grad[begin : begin + 48]
    for part in range(3):
        cols = pl.ds(pl.multiple_of(part * width + pair * WIDE, WIDE), WIDE)
        w_sc[:, part * WIDE : (part + 1) * WIDE] = w_ref[:, cols]
    total[...] += mm_nt(d_proj, w_sc[...])

    @pl.when(pair == PAIRS - 1)
    def _():
        gain = gain_row(gain_ref)
        gain_sum = jnp.zeros((1, width), F32)
        for group in range(groups):
            x = x_ref[group].astype(F32)
            d_normed = total[group * rows : (group + 1) * rows]
            factor = lax.rsqrt(jnp.mean(x * x, axis=-1, keepdims=True) + 1e-06)
            weighted = d_normed * gain
            inner = jnp.mean(weighted * x, axis=-1, keepdims=True)
            gx_ref[group] = (
                dh_ref[group] + factor * weighted - x * (factor * factor * factor) * inner
            )
            gain_sum += jnp.sum(d_normed * x * factor, axis=0, keepdims=True)
        gain_grad_ref[...] = gain_sum


def input_grads(d_proj, normed1, x, d_hidden, w_qkv, gain):
    groups, rows, width = x.shape
    whole = lambda p: (0, 0, 0)
    once = pl.Buffered(1)
    tokens = pl.BlockSpec((groups, rows, width), whole, pipeline_mode=once)
    return pl.pallas_call(
        input_grads_kernel,
        grid=(PAIRS,),
        in_specs=[
            pl.BlockSpec((groups, 1, rows, 3 * WIDE), lambda p: (0, p, 0, 0)),
            tokens,
            tokens,
            tokens,
            pl.BlockSpec(w_qkv.shape, lambda p: (0, 0), pipeline_mode=once),
            pl.BlockSpec((width,), lambda p: (0,)),
        ],
        out_specs=[
            pl.BlockSpec((1, 1, 4, 4, 48, PART), lambda p: (p % 3, p // 3, 0, 0, 0, 0)),
            tokens,
            pl.BlockSpec((1, width), lambda p: (0, 0)),
        ],
        out_shape=[
            jax.ShapeDtypeStruct((3, 2, 4, 4, 48, PART), BF16),
            jax.ShapeDtypeStruct(x.shape, F32),
            jax.ShapeDtypeStruct((1, width), F32),
        ],
        scratch_shapes=[
            pltpu.VMEM((width, groups * rows), BF16),
            pltpu.VMEM((groups * rows, width), F32),
            pltpu.VMEM((width, 3 * WIDE), BF16),
        ],
        compiler_params=params(),
        name="input_grads",
    )(d_proj.reshape(groups, PAIRS, rows, 3 * WIDE), normed1, x, d_hidden, w_qkv, gain)


def finish_kernel(
    units_ref, n1_ref, x_ref, dh_ref, w_ref, gain_ref, feed_ref, far_ref, gt_ref, gain2_ref, stats_ref,
    gx_ref, qkv_out, feed_out, small_out,
    dp_in, n1_v, n1_t, x_v, dh_v, w_v, feed_v, far_v, far_mine, far_in, dn, grads, pieces,
    core_in, here, chip_in, mine, z_in, qkv_all, feed_mine, feed_in, feed_all,
    row_own, row_in, row_sum, col_in,
    load_s, far_s, far_r, dp_s, dp_r, core_s, core_r, chip_s, chip_r, z_s, z_r, qkv_s, qkv_r, fz_s, fz_r, fa_s, fa_r,
    row_s, row_r, col_s, col_r,
):
    me = lax.axis_index("seq")
    z = lax.axis_index("batch")
    core, chip = lax.rem(me, 2), me // 2
    groups, block, width = n1_v.shape
    tokens = groups * block
    middle = tokens // 2
    chunks = pieces.shape[0]
    slots = units_ref.shape[0]
    rows = feed_in.shape[2]
    barrier = pltpu.get_barrier_semaphore()
    for bit in range(1, 8):
        pl.semaphore_signal(barrier, inc=1, device_id={"seq": me ^ bit}, device_id_type=MESH)
    for bit in range(1, 4):
        pl.semaphore_signal(barrier, inc=1, device_id={"batch": z ^ bit}, device_id_type=MESH)
    pl.semaphore_wait(barrier, 10)

    def send(source, target, sems, axis, peer):
        copy = remote(source, target, sems, axis, peer)
        copy.start()
        return copy

    across, along = me ^ 2, me ^ 4

    def spread(ref, s, r):
        return [
            send(ref.at[me], ref.at[me], (s.at[step], r.at[step]), "seq", peer)
            for step, peer in enumerate((me ^ 1, across, along))
        ]

    def relay(ref, first, s, r):
        rows = ref.shape[1]
        cut = (rows // 2 + 15) // 16 * 16
        first[1].wait()
        first[2].wait()
        upper, lower = pl.ds(0, cut), pl.ds(cut, rows - cut)
        on = [
            send(ref.at[across, upper], ref.at[across, upper], (s.at[3], r.at[3]), "seq", along),
            send(ref.at[along, lower], ref.at[along, lower], (s.at[4], r.at[4]), "seq", across),
        ]
        more = [
            send(ref.at[slot], ref.at[slot], (s.at[5 + step], r.at[5 + step]), "seq", me ^ 1)
            for step, slot in enumerate((across, along))
        ]
        return [first[0]] + more, on

    def finish_relay(ref, on, s, r):
        for copy in on:
            copy.wait()
        slot = me ^ 6
        return [send(ref.at[slot], ref.at[slot], (s.at[7], r.at[7]), "seq", me ^ 1)]

    for slot in range(slots):
        send_blocks(units_ref, dp_in, (dp_s, dp_r), slot)
    loads = [
        pltpu.make_async_copy(source, target, load_s.at[place])
        for place, (source, target) in enumerate(
            [
                (feed_ref, feed_v),
                (far_ref.at[z], far_v.at[0]),
                (n1_ref, n1_v),
                (w_ref, w_v),
                (x_ref, x_v),
                (dh_ref, dh_v),
            ]
        )
    ]
    for copy in loads:
        copy.start()
    far_z = [
        send(far_ref.at[z ^ bit], far_v.at[bit], (far_s.at[2 + bit], far_r.at[2 + bit]), "batch", z ^ bit)
        for bit in range(1, 4)
    ]

    loads[0].wait()
    for batch in range(4):
        both = feed_v[0, batch].astype(F32)
        for q in range(1, 4):
            both = both + feed_v[q, batch].astype(F32)
        feed_mine[batch] = both.astype(BF16)
    near = feed_mine.shape[1] // rows
    feed_z = [
        [
            send(
                feed_mine.at[z ^ bit, c * rows : (c + 1) * rows],
                feed_in.at[c, bit - 1],
                (fz_s.at[c, bit - 1], fz_r.at[c, bit - 1]),
                "batch",
                z ^ bit,
            )
            for bit in range(1, 4)
        ]
        for c in range(near)
    ]
    loads[2].wait()
    for group in range(groups):
        n1_t[:, group * block : (group + 1) * block] = n1_v[group].astype(F32).T.astype(BF16)
    for copy in loads[3:]:
        copy.wait()
    gain = gain_row(gain_ref)

    def unit_rows(pair, first):
        return jnp.concatenate(
            [dp_in[(first + more) * PAIRS + pair] for more in range(groups // 2)], axis=0
        )

    def pair_weights(pair):
        return jnp.concatenate(
            [
                w_v[:, pl.ds(pl.multiple_of(part * width + pair * WIDE, WIDE), WIDE)]
                for part in range(3)
            ],
            axis=1,
        )

    def input_half(first):
        gain_sum = jnp.zeros((1, width), F32)
        for more in range(groups // 2):
            group = first + more
            x = x_v[group].astype(F32)
            d_normed = dn[group * block : (group + 1) * block]
            factor = lax.rsqrt(jnp.mean(x * x, axis=-1, keepdims=True) + 1e-06)
            weighted = d_normed * gain
            inner = jnp.mean(weighted * x, axis=-1, keepdims=True)
            dh_v[group] += factor * weighted - x * (factor * factor * factor) * inner
            gain_sum += jnp.sum(d_normed * x * factor, axis=0, keepdims=True)
        return gain_sum

    for slot in range(slots):
        if (slot * GROUP) // PAIRS < groups // 2:
            wait_blocks(units_ref, dp_in, (dp_s, dp_r), slot)
    dn[...] = jnp.zeros(dn.shape, F32)

    def first_half(pair, carry):
        d_rows = unit_rows(pair, 0)
        grads[pair] = mm(n1_t[:, :middle], d_rows)
        dn[:middle] += mm_nt(d_rows, pair_weights(pair))
        return carry

    lax.fori_loop(0, PAIRS, first_half, 0)
    gain_sum = input_half(0)
    loads[1].wait()
    for copy in far_z:
        copy.wait()
    for q in range(4):
        both = far_v[0, q].astype(F32)
        for place in range(1, 4):
            both = both + far_v[place, q].astype(F32)
        far_mine[q] = both.astype(BF16)
    far_chips = [
        send(
            far_mine.at[chip ^ bit],
            far_in.at[bit - 1],
            (far_s.at[bit - 1], far_r.at[bit - 1]),
            "seq",
            me ^ (2 * bit),
        )
        for bit in range(1, 4)
    ]
    for slot in range(slots):
        if (slot * GROUP) // PAIRS >= groups // 2:
            wait_blocks(units_ref, dp_in, (dp_s, dp_r), slot)

    feed_first = []

    def spread_feed(c):
        for copy in feed_z[c] if c < near else far_chips:
            copy.wait()
        if c < near:
            both = feed_mine[z, c * rows : (c + 1) * rows].astype(F32)
            for bit in range(3):
                both = both + feed_in[c, bit].astype(F32)
        else:
            both = far_mine[chip].astype(F32)
            for bit in range(3):
                both = both + far_in[bit].astype(F32)
        feed_all[c, pl.ds(me, 1)] = both.astype(BF16)[None]
        feed_first.append(spread(feed_all.at[c], fa_s.at[c], fa_r.at[c]))

    spread_feed(0)
    to_core, to_chip = [], []

    def pass_on(c):
        to_core[c].wait()
        for q in range(4):
            both = pieces[c, core, q].astype(F32) + core_in[c, q].astype(F32)
            here[c, q] = both.astype(BF16)
        to_chip.append(
            [
                send(
                    here.at[c, q, half],
                    chip_in.at[c, place],
                    (chip_s.at[c, place], chip_r.at[c, place]),
                    "seq",
                    peer,
                )
                for place, (q, half, peer) in enumerate(
                    (
                        (chip ^ 1, first_two, across),
                        (chip ^ 3, first_two, across),
                        (chip ^ 2, last_two, along),
                        (chip ^ 3, last_two, along),
                    )
                )
            ]
        )

    first_two, last_two = pl.ds(0, 2), pl.ds(2, 2)

    def pass_again(c):
        for place, (q, half) in enumerate(
            ((chip, first_two), (chip ^ 2, first_two), (chip, last_two), (chip ^ 1, last_two))
        ):
            to_chip[c][place].wait()
            both = here[c, q, half].astype(F32) + chip_in[c, place].astype(F32)
            here[c, q, half] = both.astype(BF16)
        return [
            send(
                here.at[c, q, half],
                chip_in.at[c, place],
                (chip_s.at[c, place], chip_r.at[c, place]),
                "seq",
                peer,
            )
            for place, (q, half, peer) in (
                (4, (chip ^ 2, first_two, along)),
                (5, (chip ^ 1, last_two, across)),
            )
        ]

    for c in range(chunks):

        def second_half(side, carry, c=c):
            pair = side * chunks + c
            grad = (grads[pair] + mm(n1_t[:, middle:], unit_rows(pair, groups // 2))).astype(BF16)
            for batch in range(4):
                for q in range(4):
                    begin = batch * 192 + q * 48
                    pieces[c, side, q, batch] = grad[begin : begin + 48]
            return carry

        lax.fori_loop(0, 2, second_half, 0)
        to_core.append(
            send(
                pieces.at[c, 1 - core], core_in.at[c], (core_s.at[c], core_r.at[c]), "seq", me ^ 1
            )
        )
        if c > 0:
            pass_on(c - 1)

    def second_rows(pair, carry):
        dn[middle:] += mm_nt(unit_rows(pair, groups // 2), pair_weights(pair))
        return carry

    lax.fori_loop(0, 2, second_rows, 0)
    pass_on(chunks - 1)
    again = [pass_again(0)]
    lax.fori_loop(2, 4, second_rows, 0)
    again.append(pass_again(1))
    lax.fori_loop(4, PAIRS, second_rows, 0)
    again.append(pass_again(2))
    for c in range(1, chunks):
        spread_feed(c)
    gain_sum = gain_sum + input_half(groups // 2)
    gx_copy = pltpu.make_async_copy(dh_v, gx_ref, load_s.at[len(loads)])
    gx_copy.start()
    row_own[...] = jnp.zeros(row_own.shape, F32)
    for tap in range(3):
        for part in range(3):
            row = tap * 3 + part
            row_own[row : row + 1] = gt_ref[tap : tap + 1, part * width : (part + 1) * width]
    row_own[9:10] = gain_sum
    row_own[10:11] = gain2_ref[...]
    for place in range(4):
        row_own[11:12, place * WIDE : (place + 1) * WIDE] = stats_ref[place : place + 1]
    row_in[pl.ds(me, 1)] = row_own[...][None]
    rows_out = [
        send(row_own, row_in.at[me], (row_s.at[bit - 1], row_r.at[bit - 1]), "seq", me ^ bit)
        for bit in range(1, 8)
    ]
    to_z = []
    for c in range(chunks):
        for copy in again[c]:
            copy.wait()
        for half, place in ((first_two, 4), (last_two, 5)):
            both = here[c, chip, half].astype(F32) + chip_in[c, place].astype(F32)
            mine[c, half] = both.astype(BF16)
        to_z.append(
            [
                send(
                    mine.at[c, z ^ bit],
                    z_in.at[c, bit - 1],
                    (z_s.at[c, bit - 1], z_r.at[c, bit - 1]),
                    "batch",
                    z ^ bit,
                )
                for bit in range(1, 4)
            ]
        )
    for copy in rows_out:
        copy.wait()
    total = row_in[0]
    for place in range(1, 8):
        total = total + row_in[place]
    row_sum[...] = total
    col_in[pl.ds(z, 1)] = total[None]
    cols_out = [
        send(row_sum, col_in.at[z], (col_s.at[bit - 1], col_r.at[bit - 1]), "batch", z ^ bit)
        for bit in range(1, 4)
    ]
    last, feed_on, qkv_on = [], [], []
    for c in range(chunks):
        more, on = relay(feed_all.at[c], feed_first[c], fa_s.at[c], fa_r.at[c])
        last += more
        feed_on.append(on)
    qkv_first = []
    for c in range(chunks):
        for copy in to_z[c]:
            copy.wait()
        both = mine[c, z].astype(F32)
        for bit in range(3):
            both = both + z_in[c, bit].astype(F32)
        qkv_all[c, pl.ds(me, 1)] = both.astype(BF16)[None]
        qkv_first.append(spread(qkv_all.at[c], qkv_s.at[c], qkv_r.at[c]))
    for c in range(chunks):
        more, on = relay(qkv_all.at[c], qkv_first[c], qkv_s.at[c], qkv_r.at[c])
        last += more
        qkv_on.append(on)
    for c in range(chunks):
        last += finish_relay(feed_all.at[c], feed_on[c], fa_s.at[c], fa_r.at[c])
    for c in range(chunks):
        last += finish_relay(qkv_all.at[c], qkv_on[c], qkv_s.at[c], qkv_r.at[c])
    for copy in cols_out:
        copy.wait()
    small_out[...] = ((col_in[0] + col_in[1]) + col_in[2]) + col_in[3]
    for copy in last:
        copy.wait()
    qkv_out[...] = qkv_all[...]
    feed_out[...] = feed_all[...]
    gx_copy.wait()


def finish(units, normed1, x, d_hidden, w_qkv, gain, feed, far, grad_taps, grad_norm2, stats):
    groups, block, width = x.shape
    chunks, rows, feed_rows = 3, 48, 144
    small_shape = (16, width)
    tokens = groups * block
    slots = units.shape[0]
    vmem = pl.BlockSpec(memory_space=pltpu.VMEM)
    anywhere = pl.BlockSpec(memory_space=pl.ANY)
    pairs = [DMA((slots, GROUP)), DMA((slots, GROUP))]
    for shape in [(), (6,), (3,), (8,), (3,), (8,)]:
        pairs += [DMA((chunks,) + shape), DMA((chunks,) + shape)]
    low = lambda *shape: pltpu.VMEM(shape, BF16)
    return pl.pallas_call(
        finish_kernel,
        in_specs=[anywhere] * 5 + [vmem, anywhere, anywhere] + [vmem] * 3,
        out_specs=[anywhere, vmem, vmem, vmem],
        out_shape=[
            jax.ShapeDtypeStruct(x.shape, F32),
            jax.ShapeDtypeStruct((chunks, 8, rows, PART), BF16),
            jax.ShapeDtypeStruct((chunks, 8, feed_rows, PART), BF16),
            jax.ShapeDtypeStruct(small_shape, F32),
        ],
        scratch_shapes=[
            low(groups * PAIRS, block, 3 * WIDE),
            low(groups, block, width),
            low(width, tokens),
            low(groups, block, width),
            pltpu.VMEM((groups, block, width), F32),
            low(*w_qkv.shape),
            low(*feed.shape),
            low(*far.shape),
            low(*far.shape[1:]),
            low(3, *far.shape[2:]),
            pltpu.VMEM((tokens, width), F32),
            pltpu.VMEM((PAIRS, width, 3 * WIDE), F32),
            low(chunks, 2, 4, 4, rows, PART),
            low(chunks, 4, 4, rows, PART),
            low(chunks, 4, 4, rows, PART),
            low(chunks, 6, 2, rows, PART),
            low(chunks, 4, rows, PART),
            low(chunks, 3, rows, PART),
            low(chunks, 8, rows, PART),
            low(*feed.shape[1:]),
            low(chunks, 3, feed_rows, PART),
            low(chunks, 8, feed_rows, PART),
            pltpu.VMEM(small_shape, F32),
            pltpu.VMEM((8,) + small_shape, F32),
            pltpu.VMEM(small_shape, F32),
            pltpu.VMEM((4,) + small_shape, F32),
            DMA((7,)),
            DMA((6,)),
            DMA((6,)),
        ]
        + pairs
        + [DMA((7,)), DMA((7,)), DMA((3,)), DMA((3,))],
        compiler_params=group_params(0),
        name="finish",
    )(units, normed1, x, d_hidden, w_qkv, gain, feed, far, grad_taps, grad_norm2, stats)


def unpack_kernel(
    feed_ref, qkv_ref, small_ref, down_ref, up_ref, out_ref, grad_ref, taps_ref, gain1_ref, gain2_ref, rms_ref
):
    for r in range(2):
        rows, cols = slice(r * 96, r * 96 + 96), slice(r * PART, (r + 1) * PART)
        down_ref[rows, :PART] = feed_ref[0, r, :96].astype(F32)
        down_ref[r * 96 : r * 96 + 48, PART:] = feed_ref[0, r, 96:].astype(F32)
        down_ref[r * 96 + 48 : r * 96 + 96, PART:] = feed_ref[1, r, :48].astype(F32)
        up_ref[:96, cols] = feed_ref[1, r, 48:].astype(F32)
        up_ref[96:, cols] = feed_ref[2, r, :96].astype(F32)
        out_ref[r * 48 : r * 48 + 48] = feed_ref[2, r, 96:].astype(F32)
        for c in range(3):
            for part in range(3):
                begin = part * PAIRS * WIDE + (r * 3 + c) * WIDE
                grad_ref[:, begin : begin + WIDE] = qkv_ref[
                    c, r, :, part * WIDE : (part + 1) * WIDE
                ].astype(F32)

    @pl.when(pl.program_id(0) == 0)
    def _():
        width = small_ref.shape[1]
        for tap in range(3):
            for part in range(3):
                row = tap * 3 + part
                taps_ref[tap : tap + 1, part * width : (part + 1) * width] = small_ref[row : row + 1]
        z = lax.axis_index("batch")
        for row, ref in ((9, gain1_ref), (10, gain2_ref)):
            own = jnp.zeros((1, width // 4), F32)
            for batch in range(4):
                share = small_ref[row : row + 1, batch * width // 4 : (batch + 1) * width // 4]
                own = jnp.where(z == batch, share, own)
            ref[...] = own.reshape(ref.shape)
        count = small_ref[11:12, 3 * WIDE : 4 * WIDE]
        lane = lax.broadcasted_iota(jnp.int32, (1, WIDE), 1)
        total = jnp.zeros((1, WIDE), F32)
        for place in range(3):
            total = jnp.where(lane == place, small_ref[11:12, place * WIDE : (place + 1) * WIDE], total)
        rms_ref[...] = jnp.sqrt(total / (width * count)).reshape(rms_ref.shape)


def unpack(feed, qkv, small):
    wide = 3 * PAIRS * WIDE
    return pl.pallas_call(
        unpack_kernel,
        grid=(4,),
        in_specs=[
            pl.BlockSpec((3, 2, 144, PART), lambda i: (0, i, 0, 0)),
            pl.BlockSpec((3, 2, 48, PART), lambda i: (0, i, 0, 0)),
            pl.BlockSpec(small.shape, lambda i: (0, 0)),
        ],
        out_specs=[
            pl.BlockSpec((192, 2 * PART), lambda i: (i, 0)),
            pl.BlockSpec((192, 2 * PART), lambda i: (0, i)),
            pl.BlockSpec((96, PART), lambda i: (i % 2, i // 2)),
            pl.BlockSpec((48, wide), lambda i: (i, 0)),
            pl.BlockSpec((3, wide), lambda i: (0, 0)),
            pl.BlockSpec((192,), lambda i: (0,)),
            pl.BlockSpec((192,), lambda i: (0,)),
            pl.BlockSpec((WIDE,), lambda i: (0,)),
        ],
        out_shape=[
            jax.ShapeDtypeStruct((768, 2 * PART), F32),
            jax.ShapeDtypeStruct((192, 8 * PART), F32),
            jax.ShapeDtypeStruct((192, 2 * PART), F32),
            jax.ShapeDtypeStruct((192, wide), F32),
            jax.ShapeDtypeStruct((3, wide), F32),
            jax.ShapeDtypeStruct((192,), F32),
            jax.ShapeDtypeStruct((192,), F32),
            jax.ShapeDtypeStruct((WIDE,), F32),
        ],
        compiler_params=params(),
        name="unpack",
    )(feed, qkv, small)


def exchange(blocks):
    return lax.all_to_all(blocks, "seq", 0, 0, tiled=True)


def plain_gradients(feed, qkv):
    down = feed[:, :, :192].reshape(8, 4, 2, 96, PART).transpose(1, 0, 3, 2, 4)
    up = feed[:, :, 192:384].transpose(1, 2, 0, 3)
    out = feed[:, :, 384:].reshape(2, 4, 4, 48, PART).transpose(2, 1, 3, 0, 4)
    grad = qkv.reshape(3, 2, 4, 4, 48, 3, WIDE).transpose(3, 2, 4, 5, 1, 0, 6)
    return (
        down.reshape(3072, 768),
        up.reshape(768, 3072),
        out.reshape(768, 768),
        grad.reshape(768, 2304),
    )


def shards(
    stream_in,
    lengths,
    token_mask,
    norm1_gain,
    w_qkv,
    conv_taps,
    w_out,
    norm2_gain,
    w_up,
    w_down,
    grad_output,
):
    groups, block_len, width = stream_in.shape
    count = lax.axis_size("seq")
    batches = lax.axis_size("batch")
    units = groups * PAIRS
    slots = -(-units // count)
    spare = slots * count - units
    fitted = count == GROUP and batches == 4 and units % GROUP == 0

    def to_heads(blocks):
        blocks = jnp.pad(blocks, ((0, spare), (0, 0), (0, 0)))
        blocks = blocks.reshape((slots, count) + blocks.shape[1:])
        return jnp.stack([exchange(blocks[slot]) for slot in range(slots)])

    def to_tokens(rows):
        rows = rows.reshape(slots, count, block_len, rows.shape[2])
        return jnp.concatenate([exchange(rows[slot]) for slot in range(slots)])[:units]

    rest = (token_mask, norm2_gain, w_out, w_up, w_down)
    if fitted:
        normed1, proj, unit_out, attended, unit_lse, d_units, grad_norm2, stats, *saved = front(
            stream_in, norm1_gain, w_qkv, conv_taps, lengths, grad_output, *rest
        )
        stream_out, d_hidden, normed2, squared, d_up, d_attn, cotangent = saved
        proj = proj.reshape(slots, count * block_len, 3 * WIDE)
    else:
        normed1, proj = project(stream_in, norm1_gain, w_qkv)
        proj = to_heads(proj).reshape(slots, count * block_len, 3 * WIDE)
        unit_out, unit_lse = attend(lengths, proj, conv_taps, count)
        attended = to_tokens(unit_out)
        rest = (grad_output, token_mask, lengths) + rest[1:]
        stream_out, d_hidden, d_units, *saved = dense(stream_in, attended, *rest)
        normed2, squared, d_up, d_attn, cotangent, grad_norm2, stats = saved
        d_units = to_heads(d_units)
    d_units = d_units.reshape(slots, count * block_len, WIDE)
    saved = (squared, cotangent, normed2, d_up, attended, d_attn)
    if fitted:
        feed, far = feed_grads_send(*saved)
        same_core = [[core + 2 * chip for chip in range(4)] for core in range(2)]
        feed = lax.all_to_all(feed, "seq", 0, 0, tiled=True, axis_index_groups=same_core)
    else:
        feed = feed_grads(*saved)
    back, grad_taps = attend_back(lengths, proj, conv_taps, unit_out, d_units, unit_lse, count)

    if fitted:
        blocks = back.reshape(slots, count, block_len, 3 * WIDE)
        grad_input, qkv, feed, small = finish(
            blocks, normed1, stream_in, d_hidden, w_qkv, norm1_gain, feed, far, grad_taps, grad_norm2, stats
        )
        down, up, out, grad_qkv, taps, gain1, gain2, rms = unpack(feed, qkv, small)
        rms = rms[:3]
    else:
        pieces, grad_input, grad_norm1 = input_grads(
            to_tokens(back), normed1, stream_in, d_hidden, w_qkv, norm1_gain
        )

        def reduce(gradient):
            share = lax.psum_scatter(gradient, ("batch", "seq"), scatter_dimension=0, tiled=True)
            return lax.all_gather(share, "seq", axis=0, tiled=True).astype(F32)

        down, up, out, grad_qkv = map(reduce, plain_gradients(feed, pieces))
        small = (grad_taps[:3], grad_norm1[0], grad_norm2[0], stats[:4, 0])
        taps, gain1, gain2, stats = lax.psum(small, ("seq", "batch"))
        share = width // batches
        begin = lax.axis_index("batch") * share
        gain1, gain2 = (lax.dynamic_slice_in_dim(gain, begin, share) for gain in (gain1, gain2))
        rms = jnp.sqrt(stats[:3] / (width * stats[3]))
    return (stream_out, grad_input, gain1, grad_qkv, taps, out, gain2, up, down, rms)


def solution(mesh):
    tokens = P("batch", "seq", None)
    return jax.shard_map(
        shards,
        mesh=mesh,
        in_specs=(
            tokens,
            P("batch"),
            P("batch", "seq"),
            P(),
            P(),
            P(),
            P(),
            P(),
            P(),
            P(),
            tokens,
        ),
        out_specs=(
            tokens,
            tokens,
            P("batch"),
            P("batch", None),
            P(),
            P("batch", None),
            P("batch"),
            P("batch", None),
            P("batch", None),
            P(),
        ),
        check_vma=False,
    )
```

profile of v0, /device:TPU:0, one launch (start us, length us, event | category | flops | bytes accessed | tf_op | source)
XLA Modules:
  0.0 295.8 jit_solution(7160123583452119841)
XLA Ops:
  0.6 103.6 %front.1 = (bf16[4,256,768]{2,1,0:T(8,128)(2,1)}, bf16[3,8,256,384]{3,2,1,0:T(8,128)(2,1)}, bf16[3,2048,128]{2,1,0:T(8,128)(2,1)}, bf16[24,256,128]{2,1,0:T(8,12...) custom-call(s32[4]{0:T(128)} %lengths.3, ...), custom_call_target="tpu_custom_call" | custom-call | tf_op jit(solution)/shard_map/front/pallas_call | solution.py:807
  104.2 27.8 %feed_grads_send.1 = (bf16[4,4,288,384]{3,2,1,0:T(8,128)(2,1)}, bf16[4,4,144,384]{3,2,1,0:T(8,128)(2,1)}) custom-call(bf16[4,256,3072]{2,1,0:T(8,128)(2,1)} %get-tuple-element.49.sq_ref, bf16[4,256,768]{2,1,0:T(8,128)(2,1)} %get-tuple-element.50.cz_ref, bf16[4,256,768]{2,1,0:T(8,128)(2,1)} %get-tuple-element.51.n2_ref, ...), custom_call_target="tpu_custom_call" | custom-call | tf_op jit(solution)/shard_map/feed_grads_send/pallas_call | solution.py:1012
  132.0 4.8 %all-to-all-start = ((bf16[4,4,288,384]{3,2,1,0:T(8,128)(2,1)}), bf16[4,4,288,384]{3,2,1,0:T(8,128)(2,1)}, u32[]{:S(2)}, u32[]{:S(2)}) async-start(bf16[4,4,288,384]{3,2,1,0:T(8,128)(2,1)} %get-tuple-element.55), calls=%async_computation | async-start | bytes 7077888 | tf_op jit(solution)/shard_map/all_to_all | solution.py:1677
  136.9 28.5 %attend_back.1 = (bf16[3,2048,384]{2,1,0:T(8,128)(2,1)}, f32[8,2304]{1,0:T(8,128)}) custom-call(s32[4]{0:T(128)} %lengths.3, bf16[3,2048,384]{2,1,0:T(8,128)(2,1)} %bitcast.5, bf16[3,2304]{1,0:T(4,128)(2,1)} %taps_ref.3, bf16[3,2048,128]{2,1,0:T(8,128)(2,1)} %get-tuple-element.43.o_ref, bf16[3,2048,128]{2,1,0:T(8,128)(2,1)} %bitcast.8, ...), custom_call_target="tpu_custom_call" | custom-call | tf_op jit(solution)/shard_map/attend_back/pallas_call | solution.py:515
  165.3 14.4 %all-to-all-done.feed_ref = bf16[4,4,288,384]{3,2,1,0:T(8,128)(2,1)} async-done(((bf16[4,4,288,384]{3,2,1,0:T(8,128)(2,1)}), bf16[4,4,288,384]{3,2,1,0:T(8,128)(2,1)}, u32[]{:S(2)}, u32[]{:S(2)}) %all-to-all-start) | async-done | bytes 3538976 | tf_op jit(solution)/shard_map/all_to_all | solution.py:1677
  179.7 106.2 %finish.1 = (f32[4,256,768]{2,1,0:T(8,128)}, bf16[3,8,48,384]{3,2,1,0:T(8,128)(2,1)}, bf16[3,8,144,384]{3,2,1,0:T(8,128)(2,1)}, f32[16,768]{1,0:T(8,128)}) custom-call(bf16[3,8,256,384]{3,2,1,0:T(8,128)(2,1)} %bitcast.6, bf16[4,256,768]{2,1,0:T(8,128)(2,1)} %get-tuple-element.47.n1_ref, bf16[4,256,768]{2,1,0:T(8,128)(2,1)} %x_ref.3, ...), custom_call_target="tpu_custom_call" | custom-call | tf_op jit(solution)/shard_map/finish/pallas_call | solution.py:1486
  285.9 0.0 copy-start.1
  285.9 5.7 %unpack.1 = (f32[768,768]{1,0:T(8,128)}, f32[192,3072]{1,0:T(8,128)}, f32[192,768]{1,0:T(8,128)}, f32[192,2304]{1,0:T(8,128)}, f32[3,2304]{1,0:T(4,128)}, /*index=5*/f32[192]{0:T(256)}, f32[192]{0:T(256)}, f32[128]{0:T(128)}) custom-call(bf16[3,8,144,384]{3,2,1,0:T(8,128)(2,1)} %get-tuple-element.61.feed_ref, ...), custom_call_target="tpu_custom_call" | custom-call | tf_op jit(solution)/shard_map/unpack/pallas_call | solution.py:1576
  291.7 0.0 copy-start
  291.7 0.0 copy-done.1
  291.7 1.1 copy.23
  292.9 1.3 copy-done
  294.1 1.7 copy.24
Async XLA Ops:
  132.0 47.7 %all-to-all-start = ((bf16[4,4,288,384]{3,2,1,0:T(8,128)(2,1)}), bf16[4,4,288,384]{3,2,1,0:T(8,128)(2,1)}, u32[]{:S(2)}, u32[]{:S(2)}) async-start(bf16[4,4,288,384]{3,2,1,0:T(8,128)(2,1)} %get-tuple-element.55), calls=%async_computation | async-start | bytes 7077888 | tf_op jit(solution)/shard_map/all_to_all | solution.py:1677
  285.9 5.8 %copy-start.1 = (bf16[4,256,768]{2,1,0:T(8,128)(2,1)S(1)}, bf16[4,256,768]{2,1,0:T(8,128)(2,1)}, u32[]{:S(2)}) copy-start(bf16[4,256,768]{2,1,0:T(8,128)(2,1)} %get-tuple-element.82) | copy-start | bytes 4718596
  291.7 2.5 copy-start
where the time goes:
time: 295 us; the launch traced here: 296 us
  Pallas kernels  272 us (92%)
  waiting for transfers between devices  14.4 us (5%)
  starting transfers between devices  4.85 us (2%)
  local copies, waits for them, and re-layouts  4.11 us (1%)
    pallas_call x1, Pallas kernels, finish(): pl.pallas_call(finish_kernel, in_specs=[anywhere] * 5 + [vmem, anywhere,...  106 us
    pallas_call x1, Pallas kernels, front(): pl.pallas_call(front_kernel, in_specs=[pl.BlockSpec(memory_space=pltpu.SM...  104 us
    pallas_call x1, Pallas kernels, attend_back(): pl.pallas_call(functools.partial(attend_back_kernel, lengths.shape[0], co...  28.5 us
    pallas_call x1, Pallas kernels, feed_grads_send(): pl.pallas_call(feed_grads_send_kernel, grid=(2, 4), in_specs=[pl.BlockSpe...  27.8 us
    all_to_all x1, waiting for transfers between devices, shards(): lax.all_to_all(feed, 'seq', 0, 0, tiled=True, axis_index_groups=same_core)  14.4 us
  transfers between devices with their start and end apart: 1, of which 1 were waited for; matrix products, arithmetic and copies ran while one was open for 0% of the time, Pallas kernels for 10%

commit v1 on v0

--- a/solution.py
+++ b/solution.py
@@ -414,7 +414,7 @@
 
 
 def attend_back_kernel(
-    groups, count, lengths, p_ref, taps_ref, o_ref, do_ref, lse_ref, dp_ref, gt_ref,
+    groups, count, lengths, p_ref, taps_ref, o_ref, do_ref, lse_ref, stream_ref, dp_ref, gt_ref, stream_out_ref,
     taps, wide, q_sc, k_sc, v_sc, kt_sc, dm, dqt, s_sc, d_sc, e_sc, f_sc,
 ):
     p_ref, o_ref, do_ref, lse_ref = p_ref.at[0], o_ref.at[0], do_ref.at[0], lse_ref.at[0]
@@ -489,6 +489,7 @@
     @pl.when(pl.program_id(0) == 0)
     def _():
         gt_ref[...] = jnp.zeros(gt_ref.shape, F32)
+        stream_out_ref[...] = stream_ref[...]
 
     sums = [jnp.zeros((1, 3 * WIDE), F32) for _ in range(3)]
     for tile in range(tiles):
@@ -507,7 +508,8 @@
             gt_ref[tap : tap + 1, cols] += sums[tap][:, part * WIDE : (part + 1) * WIDE]
 
 
-def attend_back(lengths, proj, taps, attended, d_attended, lse, count):
+def attend_back(lengths, proj, taps, attended, d_attended, lse, stream, count):
+    all_rows = pl.BlockSpec(stream.shape, lambda i, lengths: (0, 0, 0), pipeline_mode=pl.Buffered(1))
     slots, rows = proj.shape[:2]
     steps = rows // BACK
     own = lambda i, lengths: (i, 0, 0)
@@ -523,10 +525,12 @@
                 pl.BlockSpec((1, rows, WIDE), own),
                 pl.BlockSpec((1, rows, WIDE), own),
                 pl.BlockSpec((1,) + lse.shape[1:], own),
+                all_rows,
             ],
             out_specs=[
                 pl.BlockSpec((1, rows, 3 * WIDE), own),
                 pl.BlockSpec((8, taps.shape[1]), whole),
+                all_rows,
             ],
             scratch_shapes=[
                 pltpu.VMEM((8, 3 * WIDE), F32),
@@ -546,10 +550,11 @@
         out_shape=[
             jax.ShapeDtypeStruct((slots, rows, 3 * WIDE), BF16),
             jax.ShapeDtypeStruct((8, taps.shape[1]), F32),
+            jax.ShapeDtypeStruct(stream.shape, stream.dtype),
         ],
         compiler_params=params(),
         name="attend_back",
-    )(lengths, proj, taps, attended, d_attended, lse)
+    )(lengths, proj, taps, attended, d_attended, lse, stream)
 
 
 def dense_kernel(
@@ -875,15 +880,10 @@
 BY_CHIP = 288
 
 
-def feed_grads_kernel(sq_ref, cz_ref, n2_ref, du_ref, att_ref, da_ref, out_ref, n2_t):
+def feed_grads_kernel(sq_ref, cz_ref, n2_ref, du_ref, att_ref, da_ref, out_ref):
     half, sub = pl.program_id(0), pl.program_id(1)
     groups, rows, width = n2_ref.shape
     tokens = groups * rows
-
-    @pl.when((half == 0) & (sub == 0))
-    def _():
-        for group in range(groups):
-            n2_t[:, group * rows : (group + 1) * rows] = n2_ref[group].astype(F32).T.astype(BF16)
 
     down = mm_tn(sq_ref[...].reshape(tokens, PART), cz_ref[...].reshape(tokens, width))
     for place in range(4):
@@ -891,7 +891,7 @@
             out_ref[place, pl.ds(sub, 1), side * 96 : side * 96 + 96] = down[
                 place * 96 : (place + 1) * 96, side * PART : (side + 1) * PART
             ].astype(BF16)[None]
-    up = mm(n2_t[...], du_ref[...].reshape(tokens, PART))
+    up = mm_tn(n2_ref[...].reshape(tokens, width), du_ref[...].reshape(tokens, PART))
     out_ref[pl.ds(sub, 1), :, 192:384] = up.astype(BF16).reshape(1, 4, 192, PART)
 
     @pl.when(sub == 0)
@@ -924,7 +924,6 @@
         ],
         out_specs=pl.BlockSpec((4, 4, 432, PART), lambda h, b: (h, 0, 0, 0)),
         out_shape=jax.ShapeDtypeStruct((8, 4, 432, PART), BF16),
-        scratch_shapes=[pltpu.VMEM((width, groups * rows), BF16)],
         compiler_params=params(),
         name="feed_grads",
     )(squared, cotangent, normed2, d_up, attended.reshape(groups, PAIRS, rows, WIDE), d_attn)
@@ -932,7 +931,7 @@
 
 def feed_grads_send_kernel(
     sq_ref, cz_ref, n2_ref, du_ref, att_ref, da_ref, chip_ref, z_ref,
-    n2_t, pieces, core_in, down_s, down_r, up_s, up_r, out_s, out_r,
+    pieces, core_in, down_s, down_r, up_s, up_r, out_s, out_r,
 ):
     half, sub = pl.program_id(0), pl.program_id(1)
     me = lax.axis_index("seq")
@@ -946,7 +945,7 @@
         pl.semaphore_wait(barrier, 1)
 
     feed_grads_kernel(
-        sq_ref, cz_ref, n2_ref, du_ref, att_ref, da_ref, pieces.at[pl.ds(half * 4, 4)], n2_t
+        sq_ref, cz_ref, n2_ref, du_ref, att_ref, da_ref, pieces.at[pl.ds(half * 4, 4)]
     )
 
     def down(part, batch, side):
@@ -1029,7 +1028,6 @@
             jax.ShapeDtypeStruct((4, 4, 432 - BY_CHIP, PART), BF16),
         ],
         scratch_shapes=[
-            pltpu.VMEM((width, groups * rows), BF16),
             pltpu.VMEM((8, 4, 432, PART), BF16),
             pltpu.VMEM(quarter, BF16),
             DMA((2, 4, 2)),
@@ -1532,8 +1530,9 @@
 
 
 def unpack_kernel(
-    feed_ref, qkv_ref, small_ref, down_ref, up_ref, out_ref, grad_ref, taps_ref, gain1_ref, gain2_ref, rms_ref
+    feed_ref, qkv_ref, small_ref, rows_ref, rows_out_ref, down_ref, up_ref, out_ref, grad_ref, taps_ref, gain1_ref, gain2_ref, rms_ref
 ):
+    rows_out_ref[...] = rows_ref[...]
     for r in range(2):
         rows, cols = slice(r * 96, r * 96 + 96), slice(r * PART, (r + 1) * PART)
         down_ref[rows, :PART] = feed_ref[0, r, :96].astype(F32)
@@ -1571,8 +1570,9 @@
         rms_ref[...] = jnp.sqrt(total / (width * count)).reshape(rms_ref.shape)
 
 
-def unpack(feed, qkv, small):
+def unpack(feed, qkv, small, rows):
     wide = 3 * PAIRS * WIDE
+    row_block = pl.BlockSpec((1,) + rows.shape[1:], lambda i: (i, 0, 0))
     return pl.pallas_call(
         unpack_kernel,
         grid=(4,),
@@ -1580,8 +1580,10 @@
             pl.BlockSpec((3, 2, 144, PART), lambda i: (0, i, 0, 0)),
             pl.BlockSpec((3, 2, 48, PART), lambda i: (0, i, 0, 0)),
             pl.BlockSpec(small.shape, lambda i: (0, 0)),
+            row_block,
         ],
         out_specs=[
+            row_block,
             pl.BlockSpec((192, 2 * PART), lambda i: (i, 0)),
             pl.BlockSpec((192, 2 * PART), lambda i: (0, i)),
             pl.BlockSpec((96, PART), lambda i: (i % 2, i // 2)),
@@ -1592,6 +1594,7 @@
             pl.BlockSpec((WIDE,), lambda i: (0,)),
         ],
         out_shape=[
+            jax.ShapeDtypeStruct(rows.shape, F32),
             jax.ShapeDtypeStruct((768, 2 * PART), F32),
             jax.ShapeDtypeStruct((192, 8 * PART), F32),
             jax.ShapeDtypeStruct((192, 2 * PART), F32),
@@ -1603,7 +1606,7 @@
         ],
         compiler_params=params(),
         name="unpack",
-    )(feed, qkv, small)
+    )(feed, qkv, small, rows)
 
 
 def exchange(blocks):
@@ -1677,14 +1680,18 @@
         feed = lax.all_to_all(feed, "seq", 0, 0, tiled=True, axis_index_groups=same_core)
     else:
         feed = feed_grads(*saved)
-    back, grad_taps = attend_back(lengths, proj, conv_taps, unit_out, d_units, unit_lse, count)
+    back, grad_taps, stream_out = attend_back(
+        lengths, proj, conv_taps, unit_out, d_units, unit_lse, stream_out, count
+    )
 
     if fitted:
         blocks = back.reshape(slots, count, block_len, 3 * WIDE)
         grad_input, qkv, feed, small = finish(
             blocks, normed1, stream_in, d_hidden, w_qkv, norm1_gain, feed, far, grad_taps, grad_norm2, stats
         )
-        down, up, out, grad_qkv, taps, gain1, gain2, rms = unpack(feed, qkv, small)
+        grad_input, down, up, out, grad_qkv, taps, gain1, gain2, rms = unpack(
+            feed, qkv, small, grad_input
+        )
         rms = rms[:3]
     else:
         pieces, grad_input, grad_norm1 = input_grads(

time: 295 us -> 292 us (0.990)
  Pallas kernels: 272 us -> 285 us
  waiting for transfers between devices: 14.4 us -> 2.09 us
  local copies, waits for them, and re-layouts: 4.11 us -> 0 us
    pallas_call x1, Pallas kernels: 28.5 us -> 40.8 us  [attend_back(): pl.pallas_call(functools.partial(attend_back_kernel, lengths.shape[0], co...]
    all_to_all x1, waiting for transfers between devices: 14.4 us -> 2.09 us  [shards(): lax.all_to_all(feed, 'seq', 0, 0, tiled=True, axis_index_groups=same_core)]
    unnamed x6 -> x0, local copies, waits for them, and re-layouts: 4.11 us -> none
  transfers between devices with their start and end apart: 1 -> 1, of which waited for: 1 -> 1; matrix products, arithmetic and copies ran while one was open for 0% -> 0% of each run, Pallas kernels for 10% -> 14%
where the time goes in v1:
time: 292 us; the launch traced here: 293 us
  Pallas kernels  285 us (98%)
  starting transfers between devices  4.85 us (2%)
    pallas_call x1, Pallas kernels, finish(): pl.pallas_call(finish_kernel, in_specs=[anywhere] * 5 + [vmem, anywhere,...  106 us
    pallas_call x1, Pallas kernels, front(): pl.pallas_call(front_kernel, in_specs=[pl.BlockSpec(memory_space=pltpu.SM...  104 us
    pallas_call x1, Pallas kernels, attend_back(): pl.pallas_call(functools.partial(attend_back_kernel, lengths.shape[0], co...  40.8 us
    pallas_call x1, Pallas kernels, feed_grads_send(): pl.pallas_call(feed_grads_send_kernel, grid=(2, 4), in_specs=[pl.BlockSpe...  27.4 us
    pallas_call x1, Pallas kernels, unpack(): pl.pallas_call(unpack_kernel, grid=(4,), in_specs=[pl.BlockSpec((3, 2, 14...  7.35 us
  transfers between devices with their start and end apart: 1, of which 1 were waited for; matrix products, arithmetic and copies ran while one was open for 0% of the time, Pallas kernels for 14%

profile of v1, /device:TPU:0, one launch (start us, length us, event | category | flops | bytes accessed | tf_op | source)
XLA Modules:
  0.0 292.7 jit_solution(4889323895648504901)
XLA Ops:
  0.6 103.6 %front.1 = (bf16[4,256,768]{2,1,0:T(8,128)(2,1)}, bf16[3,8,256,384]{3,2,1,0:T(8,128)(2,1)}, bf16[3,2048,128]{2,1,0:T(8,128)(2,1)}, bf16[24,256,128]{2,1,0:T(8,12...) custom-call(s32[4]{0:T(128)} %lengths.3, ...), custom_call_target="tpu_custom_call" | custom-call | tf_op jit(solution)/shard_map/front/pallas_call | solution.py:812
  104.2 27.4 %feed_grads_send.1 = (bf16[4,4,288,384]{3,2,1,0:T(8,128)(2,1)}, bf16[4,4,144,384]{3,2,1,0:T(8,128)(2,1)}) custom-call(bf16[4,256,3072]{2,1,0:T(8,128)(2,1)} %get-tuple-element.52.sq_ref, bf16[4,256,768]{2,1,0:T(8,128)(2,1)} %get-tuple-element.53.cz_ref, bf16[4,256,768]{2,1,0:T(8,128)(2,1)} %get-tuple-element.54.n2_ref, ...), custom_call_target="tpu_custom_call" | custom-call | tf_op jit(solution)/shard_map/feed_grads_send/pallas_call | solution.py:1011
  131.6 4.8 %all-to-all-start = ((bf16[4,4,288,384]{3,2,1,0:T(8,128)(2,1)}), bf16[4,4,288,384]{3,2,1,0:T(8,128)(2,1)}, u32[]{:S(2)}, u32[]{:S(2)}) async-start(bf16[4,4,288,384]{3,2,1,0:T(8,128)(2,1)} %get-tuple-element.58), calls=%async_computation | async-start | bytes 7077888 | tf_op jit(solution)/shard_map/all_to_all | solution.py:1680
  136.5 40.8 %attend_back.1 = (bf16[3,2048,384]{2,1,0:T(8,128)(2,1)}, f32[8,2304]{1,0:T(8,128)}, bf16[4,256,768]{2,1,0:T(8,128)(2,1)}) custom-call(s32[4]{0:T(128)} %lengths.3, bf16[3,2048,384]{2,1,0:T(8,128)(2,1)} %bitcast.5, bf16[3,2304]{1,0:T(4,128)(2,1)} %taps_ref.3, bf16[3,2048,128]{2,1,0:T(8,128)(2,1)} %get-tuple-element.44.o_ref, bf16[3,2048,128]{2,1,0:T(8,128)(2,1)} %bitcast.8, ...), custom_call_target="tpu_custom_call" | custom-call | tf_op jit(solution)/shard_map/attend_back/pallas_call | solution.py:517
  177.2 2.1 all-to-all-done.feed_ref
  179.3 105.8 %finish.1 = (f32[4,256,768]{2,1,0:T(8,128)}, bf16[3,8,48,384]{3,2,1,0:T(8,128)(2,1)}, bf16[3,8,144,384]{3,2,1,0:T(8,128)(2,1)}, f32[16,768]{1,0:T(8,128)}) custom-call(bf16[3,8,256,384]{3,2,1,0:T(8,128)(2,1)} %bitcast.6, bf16[4,256,768]{2,1,0:T(8,128)(2,1)} %get-tuple-element.50.n1_ref, bf16[4,256,768]{2,1,0:T(8,128)(2,1)} %x_ref.3, ...), custom_call_target="tpu_custom_call" | custom-call | tf_op jit(solution)/shard_map/finish/pallas_call | solution.py:1484
  285.1 7.3 %unpack.1 = (f32[4,256,768]{2,1,0:T(8,128)}, f32[768,768]{1,0:T(8,128)}, f32[192,3072]{1,0:T(8,128)}, f32[192,768]{1,0:T(8,128)}, f32[192,2304]{1,0:T(8,128)}, /...) custom-call(bf16[3,8,144,384]{3,2,1,0:T(8,128)(2,1)} %get-tuple-element.63.feed_ref, ...), custom_call_target="tpu_custom_call" | custom-call | tf_op jit(solution)/shard_map/unpack/pallas_call | solution.py:1576
Async XLA Ops:
  131.6 47.7 %all-to-all-start = ((bf16[4,4,288,384]{3,2,1,0:T(8,128)(2,1)}), bf16[4,4,288,384]{3,2,1,0:T(8,128)(2,1)}, u32[]{:S(2)}, u32[]{:S(2)}) async-start(bf16[4,4,288,384]{3,2,1,0:T(8,128)(2,1)} %get-tuple-element.58), calls=%async_computation | async-start | bytes 7077888 | tf_op jit(solution)/shard_map/all_to_all | solution.py:1680
